TPU v7x, 256 devices: a whole 4x4x8 slice. The times are simulated.
256 devices in a mesh: chan: 64 (over y, z, core), hour: 4 (over x).
Axes of the slice: x: 4, y: 4, z: 8, core: 2. Of those that a mesh axis runs over, the one named last changes fastest.
Arguments:
- spectra: bfloat16 [8, 2, 8192, 2560], P('hour', None, 'chan'), may hold values from -34 to 34, as said below
- partner_lists: int32 [64, 4], replicated, may hold values from -1 to 63, as said below
- partner_counts: int32 [64], replicated, may hold values from 2 to 4, as said below
Outputs:
- stacks: float32 [256, 8, 128, 256], P(('chan', 'hour'))
Inputs may be any that keep to these rules, and one draw needn't show every extreme that they name: The spectra are finite and bounded. `partner_lists`: row s lists distinct channel blocks, the first being s itself; entries from position partner_counts[s] on are -1. Within their counts, every block is listed by at most 4 rows, and some block by exactly 4. `partner_counts`: some row has exactly 4 partners.
All inputs are finite; a program needn't handle non-finite values.
Results may differ from a plain program's by a relative error of at most 0.0046.
Values may be sent and summed in bfloat16 or wider, within the bound.
A program may use at most 128 MiB of HBM per device.

v0:
```python
import math
import jax
import jax.numpy as jnp
from jax import lax
from jax.sharding import PartitionSpec as P

VS = 8
F0 = 64
NWIN = 8192
SMOOTH = 129
LAGS = 256


def whiten(real_part, imag_part):
    amplitude = jnp.sqrt(real_part * real_part + imag_part * imag_part)
    window_shape = (1,) * (amplitude.ndim - 1) + (SMOOTH,)
    padding = ((0, 0),) * (amplitude.ndim - 1) + ((SMOOTH // 2, SMOOTH // 2),)
    summed = lax.reduce_window(
        amplitude,
        jnp.zeros((), amplitude.dtype),
        lax.add,
        window_shape,
        (1,) * amplitude.ndim,
        padding,
    )
    denominator = summed / SMOOTH + 1e-06
    return (
        (real_part / denominator).astype(jnp.bfloat16),
        (imag_part / denominator).astype(jnp.bfloat16),
    )


def lag_table(band_bins):
    freq_index = jnp.arange(band_bins, dtype=jnp.int32)[:, None] + F0
    lag_index = jnp.arange(LAGS, dtype=jnp.int32)[None, :] - LAGS // 2
    lag_index = jnp.where(lag_index < 0, lag_index + NWIN, lag_index)
    phase_index = freq_index * lag_index % NWIN
    phase_angle = phase_index.astype(jnp.float32) * (2.0 * math.pi / NWIN)
    return jnp.concatenate([jnp.cos(phase_angle), -jnp.sin(phase_angle)], 0).astype(jnp.bfloat16)


def slot_onehot(partner_lists, partner_counts, receiver):
    offsets = jnp.arange(partner_lists.shape[1], dtype=jnp.int32)
    listed = (offsets[None, :] < partner_counts[:, None]) & (partner_lists == receiver)
    member = jnp.any(listed, axis=1)
    slot_rank = jnp.cumsum(member.astype(jnp.int32)) - 1
    slots = jnp.arange(partner_lists.shape[1], dtype=jnp.int32)
    return member[None, :] & (slot_rank[None, :] == slots[:, None])


def shards(spectra, partner_lists, partner_counts):
    windows, _, block_chans, band_bins = spectra.shape
    block_count = lax.axis_size("chan")
    hour_count = lax.axis_size("hour")
    values = spectra.astype(jnp.float32)
    white_re, white_im = whiten(values[:, 0], values[:, 1])
    stride = block_chans // VS
    local_sources = jnp.stack([white_re[:, ::stride, :], white_im[:, ::stride, :]], 1)
    local_sources = jnp.transpose(local_sources, (2, 0, 1, 3))
    receiver = lax.axis_index("chan")
    onehot = slot_onehot(partner_lists, partner_counts, receiver).astype(jnp.bfloat16)
    slot_total = onehot.shape[0]
    gathered = lax.all_gather(local_sources, "chan", axis=0, tiled=True)
    flattened = gathered.reshape(block_count, -1)
    chosen = jnp.dot(onehot, flattened, preferred_element_type=jnp.float32)
    chosen = chosen.reshape(slot_total, VS, windows, 2, band_bins)
    table_values = lag_table(band_bins)
    norm_scale = 1.0 / math.sqrt(4.0 * band_bins * windows * hour_count)

    def one_slot(source):
        cross_re = jnp.zeros((VS, block_chans, band_bins), jnp.float32)
        cross_im = jnp.zeros((VS, block_chans, band_bins), jnp.float32)
        for window in range(windows):
            src_real = source[:, window, 0][:, None, :]
            src_imag = source[:, window, 1][:, None, :]
            recv_real = white_re[window][None, :, :]
            recv_imag = white_im[window][None, :, :]
            cross_re = cross_re + src_real * recv_real + src_imag * recv_imag
            cross_im = cross_im + src_imag * recv_real - src_real * recv_imag
        cross = (
            jnp.concatenate([cross_re, cross_im], -1)
            .astype(jnp.bfloat16)
            .reshape(VS * block_chans, 2 * band_bins)
        )
        lagged = jnp.dot(cross, table_values, preferred_element_type=jnp.float32) * norm_scale
        return lagged.reshape(VS, block_chans, LAGS)

    partial_stacks = lax.map(one_slot, chosen)
    summed_hours = lax.psum(partial_stacks, "hour")
    share = slot_total // hour_count
    return lax.dynamic_slice_in_dim(summed_hours, lax.axis_index("hour") * share, share, 0)


def solution(mesh):
    return jax.shard_map(
        shards,
        mesh=mesh,
        in_specs=(P("hour", None, "chan", None), P(), P()),
        out_specs=P(("chan", "hour"), None, None, None),
        check_vma=False,
    )
```

profile of v0, /device:TPU:1, one launch (start us, length us, event | category | flops | bytes accessed | tf_op | source)
XLA Modules:
  0.0 464.1 jit_solution(17760751546049418316)
XLA Ops:
  6.5 3.2 copy.26
  9.8 0.3 convert_element_type.43
  10.1 2.3 copy-done
  12.4 0.8 add_sqrt_fusion
  13.3 129.2 %reduce_window.7 = f32[2,128,2560]{1,2,0:T(8,128)} reduce-window(f32[2,128,2560]{1,2,0:T(8,128)S(1)} %add_sqrt_fusion, f32[]{:T(128)} %constant.29.clone.1), window={size=1x1x129 pad=0_0x0_0x64_64}, to_apply=%region_2.0 | reduce-window | flops 83886080 | bytes 5242884 | tf_op jit(solution)/shard_map/reduce_window | solution.py:18
  142.4 4.0 divide_convert_fusion.1
  146.4 10.4 %slice.38 = bf16[2,8,2560]{1,2,0:T(8,128)(2,1)} slice(bf16[2,128,2560]{1,2,0:T(8,128)(2,1)S(1)} %get-tuple-element.90), slice={[0:2:1], [0:128:16], [0:2560:1]} | slice | bytes 163840 | tf_op jit(solution)/shard_map/slice | solution.py:58
  156.8 10.2 %slice.39 = bf16[2,8,2560]{1,2,0:T(8,128)(2,1)} slice(bf16[2,128,2560]{1,2,0:T(8,128)(2,1)S(1)} %get-tuple-element.91), slice={[0:2:1], [0:128:16], [0:2560:1]} | slice | bytes 163840 | tf_op jit(solution)/shard_map/slice | solution.py:58
  167.0 3.8 maximum_bitcast_fusion
  170.8 3.5 copy.27
  174.5 0.6 copy.30
  175.1 1.6 copy.31
  177.1 11.7 %cosine_convert_fusion = (bf16[2560,256]{1,0:T(8,128)(2,1)S(1)}, bf16[2560,256]{1,0:T(8,128)(2,1)S(1)}) fusion(s32[256]{0:T(256)S(1)} %compare_select_fusion, s32[2560]{0:T(1024)S(1)} %iota_add_fusion), kind=kLoop, calls=%fused_computation.34 | loop fusion | flops 11141120 | bytes 2632704 | tf_op jit(solution)/shard_map/convert.9
  188.8 1.7 pad_maximum_fusion
  190.5 74.7 %all-gather.2.cloned.1.call-done = bf16[512,2,2,2560]{3,2,1,0:T(2,128)(2,1)} async-done(((bf16[8,2,2,2560]{3,2,1,0:T(2,128)(2,1)}), bf16[512,2,2,2560]{3,2,1,0:T(2,128)(2,1)}) %all-gather.2.cloned.1.call-update) | async-done | bytes 10485776 | tf_op jit(solution)/shard_map/all_gather | solution.py:63
  265.2 13.0 %reshape.97 = bf16[64,81920]{1,0:T(8,128)(2,1)} reshape(bf16[512,2,2,2560]{3,2,1,0:T(2,128)(2,1)} %all-gather.2.cloned.1.call-done) | data formatting | bytes 20971520 | tf_op jit(solution)/shard_map/reshape | solution.py:64
  278.2 13.8 %dot_general.11 = bf16[8,2,2,2560,64]{3,2,1,0,4:T(2,128)(2,1)} reshape(bf16[81920,64]{0,1:T(8,128)(2,1)} %bitcast.71) | data formatting | bytes 20971520 | tf_op jit(solution)/shard_map/dot_general | solution.py:65
  292.0 16.1 %fusion.8 = f32[4,8,2,2,2560]{4,0,3,2,1:T(4,128)} fusion(bf16[8,2,2,2560,64]{3,2,1,0,4:T(2,128)(2,1)} %dot_general.11, s32[64]{0:T(128)S(1)} %add_reduce_fusion, pred[64]{0:T(512)(128)(4,1)S(1)} %fusion.14), kind=kOutput, calls=%fused_computation.19 | convolution fusion | flops 41943552 | bytes 11796800 | tf_op jit(solution)/shard_map/dot_general | solution.py:65
  308.2 51.6 %while.10 = (s32[]{:T(128)}, f32[4,8,128,256]{3,2,1,0:T(8,128)}, f32[4,8,2,2,2560]{4,0,3,2,1:T(4,128)}, bf16[2,128,2560]{2,1,0:T(8,128)(2,1)S(1)}, bf16[2,128,25...) while((s32[]{:T(128)}, f32[4,8,128,256]{3,2,1,0:T(8,128)}, ...), condition=%wide.region_4.5_spmd, body=%wide.region_3.4_spmd.sunk | while | flops 2748841984 | bytes 53281388 | solution.py:88
  308.5 1.7 constant_dynamic-slice_fusion.3
  310.2 0.2 copy.51
  310.3 0.2 fusion.28
  310.6 0.7 bitcast_convert_fusion.5
  311.3 5.8 %add_convert_fusion.2 = (bf16[8,128,2560]{2,1,0:T(8,128)(2,1)S(1)}, bf16[8,128,2560]{2,1,0:T(8,128)(2,1)S(1)}) fusion(f32[128,2560]{1,0:T(8,128)S(1)} %get-tuple-element.145, f32[8,2560]{1,0:T(8,128)S(1)} %get-tuple-element.148, f32[128,2560]{1,0:T(8,128)S(1)} %get-tuple-element.149, f32[8,2560]{1,0:T(8,128)S(1)} %get-tuple-element.150, ...), kind=kLoop, calls=%fused_computation.5.clone.1 | loop fusion | flops 41943040 | bytes 16056320 | tf_op jit(solution)/shard_map/convert.7
  317.1 3.1 fusion.29
  320.2 1.1 constant_dynamic-update-slice_fusion.2
  321.3 1.7 constant_dynamic-slice_fusion.3
  323.0 0.2 copy.51
  323.1 0.2 fusion.28
  323.4 0.7 bitcast_convert_fusion.5
  324.1 5.8 %add_convert_fusion.2 = (bf16[8,128,2560]{2,1,0:T(8,128)(2,1)S(1)}, bf16[8,128,2560]{2,1,0:T(8,128)(2,1)S(1)}) fusion(f32[128,2560]{1,0:T(8,128)S(1)} %get-tuple-element.145, f32[8,2560]{1,0:T(8,128)S(1)} %get-tuple-element.148, f32[128,2560]{1,0:T(8,128)S(1)} %get-tuple-element.149, f32[8,2560]{1,0:T(8,128)S(1)} %get-tuple-element.150, ...), kind=kLoop, calls=%fused_computation.5.clone.1 | loop fusion | flops 41943040 | bytes 16056320 | tf_op jit(solution)/shard_map/convert.7
  329.9 3.1 fusion.29
  333.0 1.1 constant_dynamic-update-slice_fusion.2
  334.1 1.7 constant_dynamic-slice_fusion.3
  335.8 0.2 copy.51
  336.0 0.2 fusion.28
  336.2 0.7 bitcast_convert_fusion.5
  336.9 5.8 %add_convert_fusion.2 = (bf16[8,128,2560]{2,1,0:T(8,128)(2,1)S(1)}, bf16[8,128,2560]{2,1,0:T(8,128)(2,1)S(1)}) fusion(f32[128,2560]{1,0:T(8,128)S(1)} %get-tuple-element.145, f32[8,2560]{1,0:T(8,128)S(1)} %get-tuple-element.148, f32[128,2560]{1,0:T(8,128)S(1)} %get-tuple-element.149, f32[8,2560]{1,0:T(8,128)S(1)} %get-tuple-element.150, ...), kind=kLoop, calls=%fused_computation.5.clone.1 | loop fusion | flops 41943040 | bytes 16056320 | tf_op jit(solution)/shard_map/convert.7
  342.7 3.1 fusion.29
  345.8 1.1 constant_dynamic-update-slice_fusion.2
  346.9 1.7 constant_dynamic-slice_fusion.3
  348.8 0.2 fusion.28
  349.1 0.7 bitcast_convert_fusion.5
  349.8 5.8 %add_convert_fusion.2 = (bf16[8,128,2560]{2,1,0:T(8,128)(2,1)S(1)}, bf16[8,128,2560]{2,1,0:T(8,128)(2,1)S(1)}) fusion(f32[128,2560]{1,0:T(8,128)S(1)} %get-tuple-element.145, f32[8,2560]{1,0:T(8,128)S(1)} %get-tuple-element.148, f32[128,2560]{1,0:T(8,128)S(1)} %get-tuple-element.149, f32[8,2560]{1,0:T(8,128)S(1)} %get-tuple-element.150, ...), kind=kLoop, calls=%fused_computation.5.clone.1 | loop fusion | flops 41943040 | bytes 16056320 | tf_op jit(solution)/shard_map/convert.7
  355.6 3.1 fusion.29
  358.6 1.1 constant_dynamic-update-slice_fusion.2
  359.8 94.6 %all-reduce.2.cloned.1.call-done = f32[4,8,128,256]{3,2,1,0:T(8,128)} async-done(((f32[4,8,128,256]{3,2,1,0:T(8,128)}), f32[4,8,128,256]{3,2,1,0:T(8,128)}) %all-reduce.2.cloned.1.call-update) | async-done | bytes 4194320 | tf_op jit(solution)/shard_map/psum | solution.py:89
  454.4 2.3 constant_dynamic-slice_fusion.1
  (36 shorter events, 0.7 us)
Async XLA Ops:
  6.5 258.7 %all-gather.2.cloned.1.call-start = ((), (), s32[]{:S(2)}) async-start(), calls=%async_computation | async-start | bytes 10649600 | tf_op jit(solution)/shard_map/all_gather | solution.py:63
  10.1 2.3 copy-start
  146.4 20.6 %copy-start.1 = (bf16[2,128,2560]{1,2,0:T(8,128)(2,1)}, bf16[2,128,2560]{1,2,0:T(8,128)(2,1)S(1)}, u32[]{:S(2)}) copy-start(bf16[2,128,2560]{1,2,0:T(8,128)(2,1)S(1)} %get-tuple-element.91) | copy-start | bytes 3932164
  174.4 280.0 %all-reduce.2.cloned.1.call-start = ((), (), s32[]{:S(2)}) async-start(), calls=%async_computation.1 | async-start | bytes 8388608 | tf_op jit(solution)/shard_map/psum | solution.py:89
  174.4 2.3 copy-start.3
  174.4 2.3 copy-start.4
  311.3 5.8 %copy-start.2 = (bf16[5120,256]{1,0:T(8,128)(2,1)S(1)}, bf16[5120,256]{1,0:T(8,128)(2,1)}, u32[]{:S(2)}) copy-start(bf16[5120,256]{1,0:T(8,128)(2,1)} %get-tuple-element.178) | copy-start | bytes 7864324 | tf_op jit(solution)/shard_map/while
  324.1 5.8 %copy-start.2 = (bf16[5120,256]{1,0:T(8,128)(2,1)S(1)}, bf16[5120,256]{1,0:T(8,128)(2,1)}, u32[]{:S(2)}) copy-start(bf16[5120,256]{1,0:T(8,128)(2,1)} %get-tuple-element.178) | copy-start | bytes 7864324 | tf_op jit(solution)/shard_map/while
  336.9 5.8 %copy-start.2 = (bf16[5120,256]{1,0:T(8,128)(2,1)S(1)}, bf16[5120,256]{1,0:T(8,128)(2,1)}, u32[]{:S(2)}) copy-start(bf16[5120,256]{1,0:T(8,128)(2,1)} %get-tuple-element.178) | copy-start | bytes 7864324 | tf_op jit(solution)/shard_map/while
  349.7 5.8 %copy-start.2 = (bf16[5120,256]{1,0:T(8,128)(2,1)S(1)}, bf16[5120,256]{1,0:T(8,128)(2,1)}, u32[]{:S(2)}) copy-start(bf16[5120,256]{1,0:T(8,128)(2,1)} %get-tuple-element.178) | copy-start | bytes 7864324 | tf_op jit(solution)/shard_map/while
Sparse Core Ops, SparseCore 0:
  174.5 90.6 all-gather.1
  359.9 94.4 all-reduce.1
where the time goes:
time: 467 us; the launch traced here: 464 us
  other arithmetic  178 us (38%)
  waiting for transfers between devices  169 us (36%)
  local copies, waits for them, and re-layouts  73.9 us (16%)
  matrix products  28.4 us (6%)
  between operations  14.1 us (3%)
    another operation x1, other arithmetic, whiten(): lax.reduce_window(amplitude, jnp.zeros((), amplitude.dtype), lax.add, win...  129 us
    psum x1, waiting for transfers between devices, shards(): summed_hours = lax.psum(partial_stacks, 'hour')  94.6 us
    all_gather x1, waiting for transfers between devices, shards(): gathered = lax.all_gather(local_sources, 'chan', axis=0, tiled=True)  74.7 us
    another operation x6, other arithmetic  34.9 us
    dot_general x1, matrix products, shards(): chosen = jnp.dot(onehot, flattened, preferred_element_type=jnp.float32)  16.1 us
    dot_general x1, local copies, waits for them, and re-layouts, shards(): chosen = jnp.dot(onehot, flattened, preferred_element_type=jnp.float32)  13.8 us
    reshape x1, local copies, waits for them, and re-layouts, shards(): flattened = gathered.reshape(block_count, -1)  13 us
    dot_general x4, matrix products, one_slot(): jnp.dot(cross, table_values, preferred_element_type=jnp.float32)  12.3 us
  transfers between devices with their start and end apart: 2, of which 2 were waited for; matrix products, arithmetic and copies ran while one was open for 3% of the time, Pallas kernels for 0%

commit v1 on v0

--- a/solution.py
+++ b/solution.py
@@ -9,6 +9,15 @@
 NWIN = 8192
 SMOOTH = 129
 LAGS = 256
+
+
+def add_in_pairs(array, axis):
+    size = lax.axis_size(axis)
+    summed, hop = (array, 1)
+    while hop < size:
+        summed = summed + lax.ppermute(summed, axis, [(i, i ^ hop) for i in range(size)])
+        hop = 2 * hop
+    return summed
 
 
 def whiten(real_part, imag_part):
@@ -86,7 +95,7 @@
         return lagged.reshape(VS, block_chans, LAGS)
 
     partial_stacks = lax.map(one_slot, chosen)
-    summed_hours = lax.psum(partial_stacks, "hour")
+    summed_hours = add_in_pairs(partial_stacks, "hour")
     share = slot_total // hour_count
     return lax.dynamic_slice_in_dim(summed_hours, lax.axis_index("hour") * share, share, 0)
 

time: 467 us -> 563 us (1.21)
  waiting for transfers between devices: 169 us -> 256 us
  other arithmetic: 178 us -> 185 us
    ppermute x0 -> x2, waiting for transfers between devices: none -> 181 us  [add_in_pairs(): lax.ppermute(summed, axis, [(i, i ^ hop) for i in range(size)])]
    psum x1 -> x0, waiting for transfers between devices: 94.6 us -> none  [shards(): summed_hours = lax.psum(partial_stacks, 'hour')]
    add x0 -> x2, other arithmetic: none -> 7.5 us  [add_in_pairs(): summed + lax.ppermute(summed, axis, [(i, i ^ hop) for i in range(size)])]
  transfers between devices with their start and end apart: 2 -> 3, of which waited for: 2 -> 3; matrix products, arithmetic and copies ran while one was open for 3% -> 3% of each run, Pallas kernels for 0% -> 0%
where the time goes in v1:
time: 563 us; the launch traced here: 560 us
  waiting for transfers between devices  256 us (45%)
  other arithmetic  185 us (33%)
  local copies, waits for them, and re-layouts  71.6 us (13%)
  matrix products  28.4 us (5%)
  between operations  13.7 us (2%)
    ppermute x2, waiting for transfers between devices, add_in_pairs(): lax.ppermute(summed, axis, [(i, i ^ hop) for i in range(size)])  181 us
    another operation x1, other arithmetic, whiten(): lax.reduce_window(amplitude, jnp.zeros((), amplitude.dtype), lax.add, win...  129 us
    all_gather x1, waiting for transfers between devices, shards(): gathered = lax.all_gather(local_sources, 'chan', axis=0, tiled=True)  74.8 us
    another operation x6, other arithmetic  34.9 us
    dot_general x1, matrix products, shards(): chosen = jnp.dot(onehot, flattened, preferred_element_type=jnp.float32)  16.1 us
    dot_general x1, local copies, waits for them, and re-layouts, shards(): chosen = jnp.dot(onehot, flattened, preferred_element_type=jnp.float32)  13.8 us
    reshape x1, local copies, waits for them, and re-layouts, shards(): flattened = gathered.reshape(block_count, -1)  13 us
    dot_general x4, matrix products, one_slot(): jnp.dot(cross, table_values, preferred_element_type=jnp.float32)  12.3 us
  transfers between devices with their start and end apart: 3, of which 3 were waited for; matrix products, arithmetic and copies ran while one was open for 3% of the time, Pallas kernels for 0%

profile of v1, /device:TPU:1, one launch (start us, length us, event | category | flops | bytes accessed | tf_op | source)
XLA Modules:
  0.0 559.6 jit_solution(15308878324689433575)
XLA Ops:
  6.5 3.2 copy.26
  9.8 0.3 convert_element_type.43
  10.1 2.3 copy-done
  12.4 0.8 add_sqrt_fusion
  13.3 129.3 %reduce_window.7 = f32[2,128,2560]{1,2,0:T(8,128)} reduce-window(f32[2,128,2560]{1,2,0:T(8,128)S(1)} %add_sqrt_fusion, f32[]{:T(128)} %constant.29.clone.1), window={size=1x1x129 pad=0_0x0_0x64_64}, to_apply=%region_2.0 | reduce-window | flops 83886080 | bytes 5242884 | tf_op jit(solution)/shard_map/reduce_window | solution.py:27
  142.6 4.0 divide_convert_fusion.1
  146.6 10.4 %slice.38 = bf16[2,8,2560]{1,2,0:T(8,128)(2,1)} slice(bf16[2,128,2560]{1,2,0:T(8,128)(2,1)S(1)} %get-tuple-element.90), slice={[0:2:1], [0:128:16], [0:2560:1]} | slice | bytes 163840 | tf_op jit(solution)/shard_map/slice | solution.py:67
  157.0 10.2 %slice.39 = bf16[2,8,2560]{1,2,0:T(8,128)(2,1)} slice(bf16[2,128,2560]{1,2,0:T(8,128)(2,1)S(1)} %get-tuple-element.91), slice={[0:2:1], [0:128:16], [0:2560:1]} | slice | bytes 163840 | tf_op jit(solution)/shard_map/slice | solution.py:67
  167.2 3.8 maximum_bitcast_fusion
  171.1 3.5 copy.27
  174.6 0.6 copy.30
  175.3 1.6 copy.31
  177.3 11.7 %cosine_convert_fusion = (bf16[2560,256]{1,0:T(8,128)(2,1)S(1)}, bf16[2560,256]{1,0:T(8,128)(2,1)S(1)}) fusion(s32[256]{0:T(256)S(1)} %compare_select_fusion, s32[2560]{0:T(1024)S(1)} %iota_add_fusion), kind=kLoop, calls=%fused_computation.34 | loop fusion | flops 11141120 | bytes 2632704 | tf_op jit(solution)/shard_map/convert.9
  188.9 1.7 pad_maximum_fusion
  190.7 74.8 %all-gather.2.cloned.1.call-done = bf16[512,2,2,2560]{3,2,1,0:T(2,128)(2,1)} async-done(((bf16[8,2,2,2560]{3,2,1,0:T(2,128)(2,1)}), bf16[512,2,2,2560]{3,2,1,0:T(2,128)(2,1)}) %all-gather.2.cloned.1.call-update) | async-done | bytes 10485776 | tf_op jit(solution)/shard_map/all_gather | solution.py:72
  265.5 13.0 %reshape.97 = bf16[64,81920]{1,0:T(8,128)(2,1)} reshape(bf16[512,2,2,2560]{3,2,1,0:T(2,128)(2,1)} %all-gather.2.cloned.1.call-done) | data formatting | bytes 20971520 | tf_op jit(solution)/shard_map/reshape | solution.py:73
  278.4 13.8 %dot_general.11 = bf16[8,2,2,2560,64]{3,2,1,0,4:T(2,128)(2,1)} reshape(bf16[81920,64]{0,1:T(8,128)(2,1)} %bitcast.71) | data formatting | bytes 20971520 | tf_op jit(solution)/shard_map/dot_general | solution.py:74
  292.3 16.1 %fusion.8 = f32[4,8,2,2,2560]{4,0,3,2,1:T(4,128)} fusion(bf16[8,2,2,2560,64]{3,2,1,0,4:T(2,128)(2,1)} %dot_general.11, s32[64]{0:T(128)S(1)} %add_reduce_fusion, pred[64]{0:T(512)(128)(4,1)S(1)} %fusion.14), kind=kOutput, calls=%fused_computation.19 | convolution fusion | flops 41943552 | bytes 11796800 | tf_op jit(solution)/shard_map/dot_general | solution.py:74
  308.4 51.7 %while.10 = (s32[]{:T(128)}, f32[4,8,128,256]{3,2,1,0:T(8,128)}, f32[4,8,2,2,2560]{4,0,3,2,1:T(4,128)}, bf16[2,128,2560]{2,1,0:T(8,128)(2,1)S(1)}, bf16[2,128,25...) while((s32[]{:T(128)}, f32[4,8,128,256]{3,2,1,0:T(8,128)}, ...), condition=%wide.region_4.5_spmd, body=%wide.region_3.4_spmd.sunk | while | flops 2748841984 | bytes 53281388 | solution.py:97
  308.9 1.7 constant_dynamic-slice_fusion.2
  310.8 0.2 fusion.28
  311.0 0.7 bitcast_convert_fusion.5
  311.7 5.8 %add_convert_fusion.2 = (bf16[8,128,2560]{2,1,0:T(8,128)(2,1)S(1)}, bf16[8,128,2560]{2,1,0:T(8,128)(2,1)S(1)}) fusion(f32[128,2560]{1,0:T(8,128)S(1)} %get-tuple-element.145, f32[8,2560]{1,0:T(8,128)S(1)} %get-tuple-element.148, f32[128,2560]{1,0:T(8,128)S(1)} %get-tuple-element.149, f32[8,2560]{1,0:T(8,128)S(1)} %get-tuple-element.150, ...), kind=kLoop, calls=%fused_computation.5.clone.1 | loop fusion | flops 41943040 | bytes 16056320 | tf_op jit(solution)/shard_map/convert.7
  317.5 3.1 fusion.29
  320.6 1.1 constant_dynamic-update-slice_fusion.2
  321.7 1.7 constant_dynamic-slice_fusion.2
  323.8 0.7 bitcast_convert_fusion.5
  324.5 5.8 %add_convert_fusion.2 = (bf16[8,128,2560]{2,1,0:T(8,128)(2,1)S(1)}, bf16[8,128,2560]{2,1,0:T(8,128)(2,1)S(1)}) fusion(f32[128,2560]{1,0:T(8,128)S(1)} %get-tuple-element.145, f32[8,2560]{1,0:T(8,128)S(1)} %get-tuple-element.148, f32[128,2560]{1,0:T(8,128)S(1)} %get-tuple-element.149, f32[8,2560]{1,0:T(8,128)S(1)} %get-tuple-element.150, ...), kind=kLoop, calls=%fused_computation.5.clone.1 | loop fusion | flops 41943040 | bytes 16056320 | tf_op jit(solution)/shard_map/convert.7
  330.3 3.1 fusion.29
  333.4 1.1 constant_dynamic-update-slice_fusion.2
  334.5 1.7 constant_dynamic-slice_fusion.2
  336.4 0.2 fusion.28
  336.6 0.7 bitcast_convert_fusion.5
  337.3 5.8 %add_convert_fusion.2 = (bf16[8,128,2560]{2,1,0:T(8,128)(2,1)S(1)}, bf16[8,128,2560]{2,1,0:T(8,128)(2,1)S(1)}) fusion(f32[128,2560]{1,0:T(8,128)S(1)} %get-tuple-element.145, f32[8,2560]{1,0:T(8,128)S(1)} %get-tuple-element.148, f32[128,2560]{1,0:T(8,128)S(1)} %get-tuple-element.149, f32[8,2560]{1,0:T(8,128)S(1)} %get-tuple-element.150, ...), kind=kLoop, calls=%fused_computation.5.clone.1 | loop fusion | flops 41943040 | bytes 16056320 | tf_op jit(solution)/shard_map/convert.7
  343.1 3.1 fusion.29
  346.2 1.1 constant_dynamic-update-slice_fusion.2
  347.3 1.7 constant_dynamic-slice_fusion.2
  349.2 0.2 fusion.28
  349.5 0.7 bitcast_convert_fusion.5
  350.2 5.8 %add_convert_fusion.2 = (bf16[8,128,2560]{2,1,0:T(8,128)(2,1)S(1)}, bf16[8,128,2560]{2,1,0:T(8,128)(2,1)S(1)}) fusion(f32[128,2560]{1,0:T(8,128)S(1)} %get-tuple-element.145, f32[8,2560]{1,0:T(8,128)S(1)} %get-tuple-element.148, f32[128,2560]{1,0:T(8,128)S(1)} %get-tuple-element.149, f32[8,2560]{1,0:T(8,128)S(1)} %get-tuple-element.150, ...), kind=kLoop, calls=%fused_computation.5.clone.1 | loop fusion | flops 41943040 | bytes 16056320 | tf_op jit(solution)/shard_map/convert.7
  356.0 3.1 fusion.29
  359.0 1.1 constant_dynamic-update-slice_fusion.2
  360.2 1.2 collective-permute-start
  361.4 90.9 %collective-permute-done = f32[4,8,128,256]{3,2,1,0:T(8,128)S(1)} collective-permute-done((f32[4,8,128,256]{3,2,1,0:T(8,128)}, f32[4,8,128,256]{3,2,1,0:T(8,128)S(1)}, u32[]{:S(2)}, u32[]{:S(2)}) %collective-permute-start) | collective-permute-done | bytes 4194336 | tf_op jit(solution)/shard_map/ppermute | solution.py:18
  452.3 4.9 add.101
  457.1 2.7 collective-permute-start.1
  459.9 90.1 %collective-permute-done.1 = f32[4,8,128,256]{3,2,1,0:T(8,128)} collective-permute-done((f32[4,8,128,256]{3,2,1,0:T(8,128)}, f32[4,8,128,256]{3,2,1,0:T(8,128)}, u32[]{:S(2)}, u32[]{:S(2)}) %collective-permute-start.1) | collective-permute-done | bytes 4194336 | tf_op jit(solution)/shard_map/ppermute | solution.py:18
  549.9 2.6 dynamic-slice_add_fusion
  (38 shorter events, 1.4 us)
Async XLA Ops:
  6.5 258.9 %all-gather.2.cloned.1.call-start = ((), (), s32[]{:S(2)}) async-start(), calls=%async_computation | async-start | bytes 10649600 | tf_op jit(solution)/shard_map/all_gather | solution.py:72
  10.1 2.3 copy-start
  146.6 20.7 %copy-start.1 = (bf16[2,128,2560]{1,2,0:T(8,128)(2,1)}, bf16[2,128,2560]{1,2,0:T(8,128)(2,1)S(1)}, u32[]{:S(2)}) copy-start(bf16[2,128,2560]{1,2,0:T(8,128)(2,1)S(1)} %get-tuple-element.91) | copy-start | bytes 3932164
  174.6 2.3 copy-start.3
  174.6 2.3 copy-start.4
  311.7 5.8 %copy-start.2 = (bf16[5120,256]{1,0:T(8,128)(2,1)S(1)}, bf16[5120,256]{1,0:T(8,128)(2,1)}, u32[]{:S(2)}) copy-start(bf16[5120,256]{1,0:T(8,128)(2,1)} %get-tuple-element.178) | copy-start | bytes 7864324 | tf_op jit(solution)/shard_map/while
  324.5 5.8 %copy-start.2 = (bf16[5120,256]{1,0:T(8,128)(2,1)S(1)}, bf16[5120,256]{1,0:T(8,128)(2,1)}, u32[]{:S(2)}) copy-start(bf16[5120,256]{1,0:T(8,128)(2,1)} %get-tuple-element.178) | copy-start | bytes 7864324 | tf_op jit(solution)/shard_map/while
  337.3 5.8 %copy-start.2 = (bf16[5120,256]{1,0:T(8,128)(2,1)S(1)}, bf16[5120,256]{1,0:T(8,128)(2,1)}, u32[]{:S(2)}) copy-start(bf16[5120,256]{1,0:T(8,128)(2,1)} %get-tuple-element.178) | copy-start | bytes 7864324 | tf_op jit(solution)/shard_map/while
  350.1 5.8 %copy-start.2 = (bf16[5120,256]{1,0:T(8,128)(2,1)S(1)}, bf16[5120,256]{1,0:T(8,128)(2,1)}, u32[]{:S(2)}) copy-start(bf16[5120,256]{1,0:T(8,128)(2,1)} %get-tuple-element.178) | copy-start | bytes 7864324 | tf_op jit(solution)/shard_map/while
  360.2 92.1 %collective-permute-start = (f32[4,8,128,256]{3,2,1,0:T(8,128)}, f32[4,8,128,256]{3,2,1,0:T(8,128)S(1)}, u32[]{:S(2)}, u32[]{:S(2)}) collective-permute-start(f32[4,8,128,256]{3,2,1,0:T(8,128)} %get-tuple-element.37), channel_id=1, source_target_pairs={{0,1},{1,0},{2,3},{3,2},{4,5},{5,4},{6,7},{7,6},{8,9},{9,8},{10,11... | collective-permute-start | bytes 12582920 | tf_op jit(solution)/shard_map/ppermute | solution.py:18
  457.1 92.8 %collective-permute-start.1 = (f32[4,8,128,256]{3,2,1,0:T(8,128)}, f32[4,8,128,256]{3,2,1,0:T(8,128)}, u32[]{:S(2)}, u32[]{:S(2)}) collective-permute-start(f32[4,8,128,256]{3,2,1,0:T(8,128)} %add.101), channel_id=1, source_target_pairs={{0,2},{1,3},{2,0},{3,1},{4,6},{5,7},{6,4},{7,5},{8,10},{9,11},{10,... | collective-permute-start | bytes 12582920 | tf_op jit(solution)/shard_map/ppermute | solution.py:18
Sparse Core Ops, SparseCore 0:
  174.7 90.6 all-gather.1
